TPU v7x, 512 devices: a whole 4x8x8 slice. The times are simulated.
512 devices in a mesh: row: 16 (over z, core), col: 32 (over x, y).
Axes of the slice: x: 4, y: 8, z: 8, core: 2. Of those that a mesh axis runs over, the one named last changes fastest.
Arguments:
- trail_adjoint: float32 [16384, 16384], P('row', 'col'), may hold values from -0.046875 to 0.046875
- panel: float32 [16384, 128], P('row', 'col')
- panel_adjoint: float32 [16384, 128], P('row', 'col'), may hold values from -6 to 6
- inv_diag: float32 [128, 128], replicated, as said below
- panel_index: int32 [1], replicated, may hold values from 832 to 895
Outputs:
- panel_grad: float32 [16384, 128], P('row', 'col')
- diag_grad: float32 [128, 128], P(None, 'col')
Inputs may be any that keep to these rules, and one draw needn't show every extreme that they name: inv_diag is lower triangular with a positive diagonal.
All inputs are finite; a program needn't handle non-finite values.
Results may differ from a plain program's by a relative error of at most 0.000075.
Values sent between devices are 32-bit elements; how exact they have to be, the bound alone decides.
No kernel may reach another device: no remote copies, remote signals or barrier semaphores. Data moves between devices by JAX's collectives and lax.ppermute only.
A program may use at most 64 MiB of HBM per device.

v0:
```python
import jax
import jax.numpy as jnp
from jax import lax
from jax.sharding import PartitionSpec as P


def broadcast(value, axis, root):
    mine = lax.axis_index(axis) == root
    return lax.psum(jnp.where(mine, value, jnp.zeros_like(value)), axis)


def body(trail_adjoint, panel, panel_adjoint, inv_diag, panel_index):
    rows_here, thin_cols = panel.shape
    panel_width = inv_diag.shape[0]
    ways_row = lax.axis_size("row")
    ways_col = lax.axis_size("col")
    ways_ratio = ways_col // ways_row
    col_here = lax.axis_index("col")
    index_k = panel_index[0]
    start_mod = jnp.mod(col_here - index_k - 1, ways_col)
    offset = start_mod // ways_row
    col_blocks = rows_here // (panel_width * ways_ratio)
    root_row = jnp.mod(col_here, ways_row)
    panel_rows = lax.all_gather(panel, "col", axis=1, tiled=True)
    shaped = broadcast(panel_rows, "row", root_row).reshape(
        col_blocks, ways_ratio, panel_width, panel_width
    )
    chosen = lax.dynamic_slice_in_dim(shaped, offset, 1, 1)
    column_panel = chosen.reshape(col_blocks * panel_width, panel_width)
    product = jnp.dot(
        trail_adjoint,
        column_panel,
        precision=lax.Precision.HIGHEST,
        preferred_element_type=jnp.float32,
    )
    placed = lax.dynamic_update_slice_in_dim(
        jnp.zeros((rows_here, panel_width), jnp.float32), panel_adjoint, col_here * thin_cols, 1
    )
    local_term = placed - 2.0 * product
    my_inverse = lax.dynamic_slice_in_dim(inv_diag, col_here * thin_cols, thin_cols, 1)
    contract_rows = (((0,), (0,)), ((), ()))
    thin_part = lax.psum_scatter(local_term, "col", scatter_dimension=1, tiled=True)
    full_rows = lax.all_gather(thin_part, "col", axis=1, tiled=True)
    panel_grad = jnp.dot(
        full_rows, my_inverse, precision=lax.Precision.HIGHEST, preferred_element_type=jnp.float32
    )
    gram_local = lax.dot_general(
        full_rows,
        panel,
        contract_rows,
        precision=lax.Precision.HIGHEST,
        preferred_element_type=jnp.float32,
    )
    gram_total = lax.psum(gram_local, "row")
    diag_grad = -lax.dot_general(
        inv_diag,
        gram_total,
        contract_rows,
        precision=lax.Precision.HIGHEST,
        preferred_element_type=jnp.float32,
    )
    return (panel_grad, diag_grad)


def solution(mesh):
    in_specs = (P("row", "col"), P("row", "col"), P("row", "col"), P(), P())
    out_specs = (P("row", "col"), P(None, "col"))
    return jax.shard_map(body, mesh=mesh, in_specs=in_specs, out_specs=out_specs, check_vma=False)
```

profile of v0, /device:TPU:2, one launch (start us, length us, event | category | flops | bytes accessed | tf_op | source)
XLA Modules:
  0.0 444.2 jit_solution(17022918917563937802)
XLA Ops:
  7.2 0.0 copy-start
  7.2 0.0 all-reduce.4.cloned.1.call-start
  7.2 52.3 %all-gather = f32[32,4,1024]{2,1,0:T(4,128)S(1)} all-gather(f32[1,4,1024]{2,1,0:T(4,128)} %bitcast.33), channel_id=1, replica_groups=mesh['row'=16,'col'=32] {'col'}, dimensions={0}, use_global_device_ids=true | all-gather | bytes 540672 | tf_op jit(solution)/shard_map/all_gather | solution.py:24
  59.5 0.0 copy-start.3
  59.5 0.1 broadcast_select_fusion
  59.7 0.2 reshape.18
  59.9 1.2 reshape.10
  61.1 0.0 all-reduce.4.cloned.1.call-update
  61.1 0.0 all-reduce.6.cloned.1.call-start
  61.9 0.0 copy-done.3
  62.0 115.0 %all-reduce.4.cloned.1.call-done = f32[4,2,128,128]{2,1,0,3:T(2,128)} async-done(((f32[4,2,128,128]{2,1,0,3:T(2,128)}), f32[4,2,128,128]{2,1,0,3:T(2,128)}) %all-reduce.4.cloned.1.call-update) | async-done | bytes 524304 | tf_op jit(solution)/shard_map/psum | solution.py:9
  177.0 1.9 dynamic-slice_reduce_fusion
  178.8 0.0 copy-done
  178.8 0.0 copy-start.2
  178.9 3.1 fusion.1
  182.0 0.0 copy-start.1
  182.0 0.0 all-reduce.6.cloned.1.call-update
  182.0 1.3 dynamic-slice
  183.9 155.1 %all-reduce.6.cloned.1.call-done = f32[1024,128]{0,1:T(8,128)} async-done(((f32[1024,128]{0,1:T(8,128)}), f32[1024,128]{0,1:T(8,128)}) %all-reduce.6.cloned.1.call-update) | async-done | bytes 524304
  339.1 0.8 dynamic-slice_bitcast_fusion
  339.8 48.1 %all-gather.1 = f32[32,4,1024]{2,1,0:T(4,128)S(1)} all-gather(f32[1,4,1024]{2,1,0:T(4,128)S(1)} %dynamic-slice_bitcast_fusion), channel_id=1, replica_groups=mesh['row'=16,'col'=32] {'col'}, dimensions={0}, use_global_device_ids=true | all-gather | bytes 540672 | tf_op jit(solution)/shard_map/all_gather | solution.py:43
  387.9 0.2 reshape.15
  388.1 0.0 copy-done.2
  388.1 0.5 fusion.8
  388.6 46.8 %psum.15 = f32[128,4]{1,0:T(8,128)S(1)} all-reduce(f32[128,4]{1,0:T(8,128)S(1)} %fusion.8), channel_id=1, replica_groups=mesh['row'=16,'col'=32] {'row'}, use_global_device_ids=true, to_apply=%region_2.3 | all-reduce | flops 512 | bytes 4096 | tf_op jit(solution)/shard_map/psum | solution.py:54
  435.4 0.0 copy-done.1
  435.4 1.0 fusion.5
  436.5 0.8 fusion.2
  (2 shorter events, 0.1 us)
Async XLA Ops:
  7.2 171.7 %copy-start = (f32[1024,512]{1,0:T(8,128)S(1)}, f32[1024,512]{1,0:T(8,128)}, u32[]{:S(2)}) copy-start(f32[1024,512]{1,0:T(8,128)} %param.5) | copy-start | bytes 6291460
  7.2 169.8 %all-reduce.4.cloned.1.call-start = ((), (), s32[]{:S(2)}) async-start(), calls=%async_computation | async-start | bytes 1048576 | tf_op jit(solution)/shard_map/psum | solution.py:9
  59.5 2.4 copy-start.3
  61.1 277.9 %all-reduce.6.cloned.1.call-start = ((), (), s32[]{:S(2)}) async-start(), calls=%async_computation.1 | async-start | bytes 1048576
  178.8 209.2 %copy-start.2 = (f32[1024,4]{0,1:T(4,128)S(1)}, f32[1024,4]{0,1:T(4,128)}, u32[]{:S(2)}) copy-start(f32[1024,4]{0,1:T(4,128)} %param.6) | copy-start | bytes 49156
  182.0 253.5 %copy-start.1 = (f32[128,128]{1,0:T(8,128)S(1)}, f32[128,128]{1,0:T(8,128)}, u32[]{:S(2)}) copy-start(f32[128,128]{1,0:T(8,128)} %param.8) | copy-start | bytes 196612
Sparse Core Ops, SparseCore 0:
  61.3 115.6 all-reduce.3
  182.1 156.9 all-reduce.5
where the time goes:
time: 445 us; the launch traced here: 444 us
  waiting for transfers between devices  270 us (61%)
  blocking collectives  147 us (33%)
  between operations  15.5 us (3%)
  local copies, waits for them, and re-layouts  5.58 us (1%)
  matrix products  5.52 us (1%)
    unnamed x3, waiting for transfers between devices  155 us
    psum x1, waiting for transfers between devices, broadcast(): return lax.psum(jnp.where(mine, value, jnp.zeros_like(value)), axis)  115 us
    all_gather x1, blocking collectives, body(): panel_rows = lax.all_gather(panel, 'col', axis=1, tiled=True)  52.3 us
    all_gather x1, blocking collectives, body(): full_rows = lax.all_gather(thin_part, 'col', axis=1, tiled=True)  48.1 us
    psum x1, blocking collectives, body(): gram_total = lax.psum(gram_local, 'row')  46.8 us
  transfers between devices with their start and end apart: 2, of which 2 were waited for; matrix products, arithmetic and copies ran while one was open for 0% of the time, Pallas kernels for 0%

commit v1 on v0

--- a/solution.py
+++ b/solution.py
@@ -51,7 +51,7 @@
         precision=lax.Precision.HIGHEST,
         preferred_element_type=jnp.float32,
     )
-    gram_total = lax.psum(gram_local, "row")
+    gram_total = jnp.sum(jax.lax.all_gather(gram_local, "row"), 0)
     diag_grad = -lax.dot_general(
         inv_diag,
         gram_total,

time: 445 us -> 418 us (0.939)
  the two profiles are of different devices: /device:TPU:2 before, /device:TPU:1 now
where the time goes in v1:
time: 418 us
  waiting for transfers between devices  280 us (67%)
  blocking collectives  111 us (27%)
  between operations  15.5 us (4%)
  local copies, waits for them, and re-layouts  5.58 us (1%)
  matrix products  5.41 us (1%)
    unnamed x3, waiting for transfers between devices  152 us
    psum x1, waiting for transfers between devices, broadcast(): return lax.psum(jnp.where(mine, value, jnp.zeros_like(value)), axis)  128 us
    all_gather x1, blocking collectives, body(): panel_rows = lax.all_gather(panel, 'col', axis=1, tiled=True)  40 us
    all_gather x1, blocking collectives, body(): full_rows = lax.all_gather(thin_part, 'col', axis=1, tiled=True)  36 us
    all_gather x1, blocking collectives, body(): gram_total = jnp.sum(jax.lax.all_gather(gram_local, 'row'), 0)  35.1 us
  transfers between devices with their start and end apart: 2, of which 2 were waited for; matrix products, arithmetic and copies ran while one was open for 0% of the time, Pallas kernels for 0%

profile of v1, /device:TPU:1, one launch (start us, length us, event | category | flops | bytes accessed | tf_op | source)
XLA Modules:
  0.0 417.7 jit_solution(14441229577438762019)
XLA Ops:
  7.2 0.0 copy-start
  7.2 0.0 all-reduce.4.cloned.1.call-start
  7.2 40.0 %all-gather.1 = f32[32,4,1024]{2,1,0:T(4,128)S(1)} all-gather(f32[1,4,1024]{2,1,0:T(4,128)} %bitcast.39), channel_id=1, replica_groups=mesh['row'=16,'col'=32] {'col'}, dimensions={0}, use_global_device_ids=true | all-gather | bytes 540672 | tf_op jit(solution)/shard_map/all_gather | solution.py:24
  47.2 0.0 copy-start.3
  47.2 0.1 broadcast_select_fusion
  47.3 0.2 reshape.19
  47.5 1.2 reshape.10
  48.8 0.0 all-reduce.4.cloned.1.call-update
  48.8 0.0 all-reduce.6.cloned.1.call-start
  49.6 0.0 copy-done.3
  49.6 128.2 %all-reduce.4.cloned.1.call-done = f32[4,2,128,128]{2,1,0,3:T(2,128)} async-done(((f32[4,2,128,128]{2,1,0,3:T(2,128)}), f32[4,2,128,128]{2,1,0,3:T(2,128)}) %all-reduce.4.cloned.1.call-update) | async-done | bytes 524304 | tf_op jit(solution)/shard_map/psum | solution.py:9
  177.8 1.9 dynamic-slice_reduce_fusion
  179.6 0.0 copy-done
  179.7 0.0 copy-start.2
  179.7 3.1 fusion.1
  182.8 0.0 copy-start.1
  182.8 0.0 all-reduce.6.cloned.1.call-update
  182.8 1.3 dynamic-slice
  184.7 151.8 %all-reduce.6.cloned.1.call-done = f32[1024,128]{0,1:T(8,128)} async-done(((f32[1024,128]{0,1:T(8,128)}), f32[1024,128]{0,1:T(8,128)}) %all-reduce.6.cloned.1.call-update) | async-done | bytes 524304
  336.5 0.8 dynamic-slice_bitcast_fusion
  337.3 36.0 %all-gather.2 = f32[32,4,1024]{2,1,0:T(4,128)S(1)} all-gather(f32[1,4,1024]{2,1,0:T(4,128)S(1)} %dynamic-slice_bitcast_fusion), channel_id=1, replica_groups=mesh['row'=16,'col'=32] {'col'}, dimensions={0}, use_global_device_ids=true | all-gather | bytes 540672 | tf_op jit(solution)/shard_map/all_gather | solution.py:43
  373.2 0.2 reshape.16
  373.4 0.0 copy-done.2
  373.4 0.5 fusion.8
  373.9 35.1 %all-gather = f32[2048,4]{0,1:T(4,128)S(1)} all-gather(f32[128,4]{0,1:T(4,128)S(1)} %fusion.8), channel_id=2, replica_groups=mesh['row'=16,'col'=32] {'row'}, dimensions={0}, use_global_device_ids=true | all-gather | bytes 34816 | tf_op jit(solution)/shard_map/all_gather | solution.py:54
  409.1 0.0 copy-done.1
  409.1 1.1 fusion.5
  410.1 0.7 fusion.2
  (3 shorter events, 0.1 us)
Async XLA Ops:
  7.2 172.5 %copy-start = (f32[1024,512]{1,0:T(8,128)S(1)}, f32[1024,512]{1,0:T(8,128)}, u32[]{:S(2)}) copy-start(f32[1024,512]{1,0:T(8,128)} %param.5) | copy-start | bytes 6291460
  7.2 170.6 %all-reduce.4.cloned.1.call-start = ((), (), s32[]{:S(2)}) async-start(), calls=%async_computation | async-start | bytes 1048576 | tf_op jit(solution)/shard_map/psum | solution.py:9
  47.2 2.4 copy-start.3
  48.8 287.7 %all-reduce.6.cloned.1.call-start = ((), (), s32[]{:S(2)}) async-start(), calls=%async_computation.1 | async-start | bytes 1048576
  179.7 193.8 %copy-start.2 = (f32[1024,4]{0,1:T(4,128)S(1)}, f32[1024,4]{0,1:T(4,128)}, u32[]{:S(2)}) copy-start(f32[1024,4]{0,1:T(4,128)} %param.6) | copy-start | bytes 49156
  182.8 226.3 %copy-start.1 = (f32[128,128]{1,0:T(8,128)S(1)}, f32[128,128]{1,0:T(8,128)}, u32[]{:S(2)}) copy-start(f32[128,128]{1,0:T(8,128)} %param.8) | copy-start | bytes 196612
Sparse Core Ops, SparseCore 0:
  48.9 128.8 all-reduce.3
  182.9 153.5 all-reduce.5
